TPU v7x, 128 devices: a whole 4x4x4 slice. The times are simulated.
128 devices in a mesh: aa: 16 (over x, z), ba: 8 (over y, core).
Axes of the slice: x: 4, y: 4, z: 4, core: 2. Of those that a mesh axis runs over, the one named last changes fastest.
Arguments:
- tokens: bfloat16 [16384, 1024], P(('aa', 'ba')), may hold values from -24 to 24, as said below
- attn_gain: float32 [1024], replicated, may hold values from 0.25 to 1.75
- w_query: bfloat16 [1024, 1024], replicated, may hold values from -0.1875 to 0.1875
- w_key: bfloat16 [1024, 1024], replicated, may hold values from -0.1875 to 0.1875
- w_value: bfloat16 [1024, 1024], replicated, may hold values from -0.1875 to 0.1875
- head_gain: float32 [1024], P('ba'), may hold values from 0.25 to 1.75
- w_output: bfloat16 [1024, 1024], replicated, may hold values from -0.1875 to 0.1875
- mlp_gain: float32 [1024], replicated, may hold values from 0.25 to 1.75
- w_in: bfloat16 [1024, 4096], replicated, may hold values from -0.1875 to 0.1875
- w_out: bfloat16 [4096, 1024], replicated, may hold values from -0.09375 to 0.09375
Outputs:
- attended: bfloat16 [16384, 1024], P(('aa', 'ba'))
- result: bfloat16 [16384, 1024], P(('aa', 'ba'))
Inputs may be any that keep to these rules, and one draw needn't show every extreme that they name: `tokens`: entries have magnitude at most 24.
All inputs are finite; a program needn't handle non-finite values.
Results may differ from a plain program's by a relative error of at most 0.013.
Values may be sent and summed in bfloat16 or wider, within the bound.
No kernel may reach another device: no remote copies, remote signals or barrier semaphores. Data moves between devices by JAX's collectives and lax.ppermute only.
A program may use at most 128 MiB of HBM per device.

v0:
```python
import jax
import jax.numpy as jnp
from jax import lax
from jax.sharding import Mesh
from jax.sharding import PartitionSpec as P

D = 1024
H = 16
AA = ("aa_0", "aa_1")
AA_BA = ("aa_0", "aa_1", "ba")


def neutral_like(shard, identity):
    return jnp.zeros_like(shard) + jnp.asarray(identity, shard.dtype)


def prefix_by_axis(shard, axes, combine, identity):
    before = start = neutral_like(shard, identity)
    subtotal = shard
    for axis in reversed(axes):
        length, index = (lax.axis_size(axis), lax.axis_index(axis))
        pieces = lax.all_gather(subtotal.astype(jnp.bfloat16), axis)
        inside, subtotal = (start, start)
        for k in range(length):
            passed = k < index
            subtotal = combine(subtotal, pieces[k].astype(shard.dtype))
            inside = jnp.where(passed, subtotal, inside)
        before = combine(inside, before)
    return before


def rms_scale(matrix, scale_vec):
    matrix = matrix.astype(jnp.float32)
    return matrix * lax.rsqrt(jnp.mean(matrix * matrix, axis=-1, keepdims=True) + 1e-05) * scale_vec


def outer_features(vectors):
    length, head_count, head_size = vectors.shape
    return (vectors[..., :, None] * vectors[..., None, :]).reshape(
        length, head_count, head_size * head_size
    )


def features(vectors):
    return outer_features(vectors).astype(jnp.bfloat16)


def add_states(earlier_state, later_state):
    return earlier_state + later_state


def body(tokens, attn_gain, w_query, w_key, w_value, head_gain, w_output, mlp_gain, w_in, w_out):
    normed = rms_scale(tokens, attn_gain).astype(jnp.bfloat16)
    query_loc = jnp.dot(normed, w_query, preferred_element_type=jnp.float32).astype(jnp.bfloat16)
    keys_loc = jnp.dot(normed, w_key, preferred_element_type=jnp.float32).astype(jnp.bfloat16)
    values_loc = jnp.dot(normed, w_value, preferred_element_type=jnp.float32).astype(jnp.bfloat16)
    queries, keys, values = (
        lax.all_to_all(query_loc, "ba", split_axis=1, concat_axis=0, tiled=True),
        lax.all_to_all(keys_loc, "ba", split_axis=1, concat_axis=0, tiled=True),
        lax.all_to_all(values_loc, "ba", split_axis=1, concat_axis=0, tiled=True),
    )
    head_size = D // H
    length = queries.shape[0]
    head_count = queries.shape[1] // head_size
    block_len = min(512, length)
    blocks = length // block_len

    def shaped(matrix):
        return matrix.reshape(blocks, block_len, head_count, head_size)

    causal = jnp.arange(block_len)[:, None] >= jnp.arange(block_len)[None, :]

    def local_pass(carry_state, block_in):
        query_blk, key_blk, value_blk = block_in
        scores = jnp.einsum("ihd,jhd->hij", query_blk, key_blk, preferred_element_type=jnp.float32)
        weights = jnp.where(causal[None], scores * scores, 0.0).astype(jnp.bfloat16)
        inside = jnp.einsum("hij,jhd->ihd", weights, value_blk, preferred_element_type=jnp.float32)
        key_feat = features(key_blk.astype(jnp.float32))
        grown_state = carry_state + jnp.einsum(
            "jhf,jhd->fhd", key_feat, value_blk, preferred_element_type=jnp.float32
        )
        return (grown_state, (inside, carry_state))

    feat_count = features(jnp.zeros((1, 1, head_size), jnp.float32)).shape[-1]
    start_state = jnp.zeros((feat_count, head_count, head_size), jnp.float32)
    local_total, (inside_all, before_all) = lax.scan(
        local_pass, start_state, (shaped(queries), shaped(keys), shaped(values))
    )
    flat_total = local_total.reshape(feat_count, head_count * head_size)
    earlier = prefix_by_axis(flat_total, AA, add_states, jnp.zeros_like(flat_total))
    earlier = earlier.reshape(feat_count, head_count, head_size)

    def apply_pass(block_in):
        query_blk, inside, before = block_in
        query_feat = features(query_blk.astype(jnp.float32))
        state_bf = (before + earlier).astype(jnp.bfloat16)
        carried = jnp.einsum(
            "ihf,fhd->ihd", query_feat, state_bf, preferred_element_type=jnp.float32
        )
        return inside + carried

    numerator = lax.map(apply_pass, (shaped(queries), inside_all, before_all)).reshape(
        length, head_count, head_size
    )
    scaled = numerator * lax.rsqrt(jnp.mean(numerator * numerator, axis=-1, keepdims=True) + 1e-05)
    scaled = scaled * head_gain.reshape(head_count, head_size)
    attended_heads = scaled.reshape(length, head_count * head_size).astype(jnp.bfloat16)
    attended = lax.all_to_all(attended_heads, "ba", split_axis=0, concat_axis=1, tiled=True)
    stream = (
        tokens.astype(jnp.float32) + jnp.dot(attended, w_output, preferred_element_type=jnp.float32)
    ).astype(jnp.bfloat16)
    normed_mlp = rms_scale(stream, mlp_gain).astype(jnp.bfloat16)
    hidden = jax.nn.gelu(
        jnp.dot(normed_mlp, w_in, preferred_element_type=jnp.float32), approximate=True
    ).astype(jnp.bfloat16)
    result = (
        stream.astype(jnp.float32) + jnp.dot(hidden, w_out, preferred_element_type=jnp.float32)
    ).astype(jnp.bfloat16)
    return (attended, result)


def solution(mesh):
    finer = Mesh(mesh.devices.reshape(4, 4, mesh.shape["ba"]), ("aa_0", "aa_1", "ba"))
    placed = (P(AA_BA, None), P(), P(), P(), P(), P("ba"), P(), P(), P(), P())
    return jax.shard_map(
        body,
        mesh=finer,
        in_specs=placed,
        out_specs=(P(AA_BA, None), P(AA_BA, None)),
        check_vma=False,
    )
```

profile of v0, /device:TPU:1, one launch (start us, length us, event | category | flops | bytes accessed | tf_op | source)
XLA Modules:
  0.0 256.1 jit_solution(17409837083859735016)
XLA Ops:
  7.2 1.2 fusion.54
  8.4 2.2 convolution_convert_fusion
  11.5 6.0 %all-to-all-start.2 = ((bf16[128,8,128]{0,2,1:T(8,128)(2,1)}), bf16[128,8,128]{0,2,1:T(8,128)(2,1)S(1)}, u32[]{:S(2)}, u32[]{:S(2)}) async-start(bf16[128,8,128]{0,2,1:T(8,128)(2,1)} %bitcast.11), calls=%async_computation.2 | async-start | bytes 524288 | tf_op jit(solution)/shard_map/all_to_all | solution.py:58
  17.5 2.1 convolution_convert_fusion.2
  20.4 3.5 %all-to-all-done.2 = bf16[128,8,128]{0,2,1:T(8,128)(2,1)S(1)} async-done(((bf16[128,8,128]{0,2,1:T(8,128)(2,1)}), bf16[128,8,128]{0,2,1:T(8,128)(2,1)S(1)}, u32[]{:S(2)}, u32[]{:S(2)}) %all-to-all-start.2) | async-done | bytes 262176 | tf_op jit(solution)/shard_map/all_to_all | solution.py:58
  23.9 4.4 %all-to-all-start = ((bf16[128,8,128]{0,2,1:T(8,128)(2,1)}), bf16[128,8,128]{0,2,1:T(8,128)(2,1)S(1)}, u32[]{:S(2)}, u32[]{:S(2)}) async-start(bf16[128,8,128]{0,2,1:T(8,128)(2,1)} %bitcast.7), calls=%async_computation | async-start | bytes 524288 | tf_op jit(solution)/shard_map/all_to_all | solution.py:60
  28.3 2.1 convolution_convert_fusion.1
  31.2 3.6 %all-to-all-done = bf16[128,8,128]{0,2,1:T(8,128)(2,1)S(1)} async-done(((bf16[128,8,128]{0,2,1:T(8,128)(2,1)}), bf16[128,8,128]{0,2,1:T(8,128)(2,1)S(1)}, u32[]{:S(2)}, u32[]{:S(2)}) %all-to-all-start) | async-done | bytes 262176 | tf_op jit(solution)/shard_map/all_to_all | solution.py:60
  34.8 4.4 %all-to-all-start.1 = ((bf16[128,8,128]{0,2,1:T(8,128)(2,1)}), bf16[128,8,128]{0,2,1:T(8,128)(2,1)S(1)}, u32[]{:S(2)}, u32[]{:S(2)}) async-start(bf16[128,8,128]{0,2,1:T(8,128)(2,1)} %bitcast.9), calls=%async_computation.1 | async-start | bytes 524288 | tf_op jit(solution)/shard_map/all_to_all | solution.py:59
  40.5 5.1 %all-to-all-done.1 = bf16[128,8,128]{0,2,1:T(8,128)(2,1)S(1)} async-done(((bf16[128,8,128]{0,2,1:T(8,128)(2,1)}), bf16[128,8,128]{0,2,1:T(8,128)(2,1)S(1)}, u32[]{:S(2)}, u32[]{:S(2)}) %all-to-all-start.1) | async-done | bytes 262176 | tf_op jit(solution)/shard_map/all_to_all | solution.py:59
  46.7 25.1 %while.26 = (s32[]{:T(128)}, f32[4096,2,64]{0,2,1:T(8,128)}, f32[2,512,2,64]{1,3,2,0:T(8,128)S(1)}, f32[2,4096,2,64]{1,3,2,0:T(8,128)}, bf16[2,512,2,64]{1,3,2,0...) while((s32[]{:T(128)}, f32[4096,2,64]{0,2,1:T(8,128)}, ...), condition=%wide.region_2.3_spmd.clone, body=%wide.region_1.2_spmd.clone.sunk | while | flops 682950656 | bytes 43911844 | solution.py:86
  46.7 1.6 bitcast_dynamic-update-slice_fusion.2
  49.2 3.3 %multiply_convert_fusion.11 = bf16[512,2,64,64]{0,3,2,1:T(8,128)(2,1)S(1)} fusion(f32[512,2,64]{0,2,1:T(8,128)S(1)} %bitcast_convert_fusion.5), kind=kLoop, calls=%fused_computation.10.clone.1 | loop fusion | flops 8388608 | bytes 8650752 | tf_op jit(solution)/shard_map/while/body/eval_jaxpr/convert_element_type | solution.py:45
  52.5 2.8 %fusion.100 = f32[4096,2,64]{0,2,1:T(8,128)S(1)} fusion(bf16[512,2,4096]{0,2,1:T(8,128)(2,1)S(1)} %bitcast.123, f32[4096,2,64]{0,2,1:T(8,128)S(1)} %copy-done.1, pred[]{:T(512)S(6)} %compare.3, bf16[2,512,2,64]{1,3,2,0:T(8,128)(2,1)S(1)} %get-tuple-element.310, s32[]{:T(128)} %get-tuple-element.297), kind=kOutput, calls=%fused_computation.12.clone.1 | convolution fusion | flops 537919488 | bytes 12713989 | tf_op jit(solution)/shard_map/while/body/eval_jaxpr/jhf,jhd->fhd/dot_general | solution.py:79
  55.3 1.3 copy-done.2
  56.7 1.7 fusion.101
  58.5 3.1 %bitcast_dynamic-update-slice_fusion.2 = f32[2,4096,2,64]{1,3,2,0:T(8,128)} fusion(f32[2,4096,2,64]{1,3,2,0:T(8,128)} %get-tuple-element.300, s32[]{:T(128)} %get-tuple-element.297, f32[4096,2,64]{0,2,1:T(8,128)} %get-tuple-element.298, pred[]{:T(512)S(6)} %compare.3), kind=kLoop, calls=%fused_computation.13.clone.1 | loop fusion | flops 524288 | bytes 4194817 | tf_op jit(solution)/shard_map/while/body/jit(dynamic_update_index_in_dim)/dynamic_update_slice | solution.py:86
  62.5 3.3 %multiply_convert_fusion.11 = bf16[512,2,64,64]{0,3,2,1:T(8,128)(2,1)S(1)} fusion(f32[512,2,64]{0,2,1:T(8,128)S(1)} %bitcast_convert_fusion.5), kind=kLoop, calls=%fused_computation.10.clone.1 | loop fusion | flops 8388608 | bytes 8650752 | tf_op jit(solution)/shard_map/while/body/eval_jaxpr/convert_element_type | solution.py:45
  65.8 2.8 %fusion.100 = f32[4096,2,64]{0,2,1:T(8,128)S(1)} fusion(bf16[512,2,4096]{0,2,1:T(8,128)(2,1)S(1)} %bitcast.123, f32[4096,2,64]{0,2,1:T(8,128)S(1)} %copy-done.1, pred[]{:T(512)S(6)} %compare.3, bf16[2,512,2,64]{1,3,2,0:T(8,128)(2,1)S(1)} %get-tuple-element.310, s32[]{:T(128)} %get-tuple-element.297), kind=kOutput, calls=%fused_computation.12.clone.1 | convolution fusion | flops 537919488 | bytes 12713989 | tf_op jit(solution)/shard_map/while/body/eval_jaxpr/jhf,jhd->fhd/dot_general | solution.py:79
  68.6 1.3 copy-done.2
  70.0 1.7 fusion.101
  71.8 2.9 %convert_element_type.145 = bf16[4096,2,64]{0,2,1:T(8,128)(2,1)} convert(f32[4096,2,64]{0,2,1:T(8,128)} %get-tuple-element.80) | non-fusion elementwise | flops 524288 | bytes 3145728 | tf_op jit(solution)/shard_map/convert_element_type | solution.py:22
  74.7 2.3 copy.64
  77.2 48.9 %all-gather.3.cloned.1.call-done = bf16[4,4096,128]{2,1,0:T(8,128)(2,1)} async-done(((bf16[1,4096,128]{2,1,0:T(8,128)(2,1)}), bf16[4,4096,128]{2,1,0:T(8,128)(2,1)}) %all-gather.3.cloned.1.call-update) | async-done | bytes 4194320 | tf_op jit(solution)/shard_map/all_gather | solution.py:22
  126.1 4.2 %fusion.72 = (bf16[1,4096,128]{2,1,0:T(8,128)(2,1)}, bf16[1,4096,128]{2,1,0:T(8,128)(2,1)}, bf16[1,4096,128]{2,1,0:T(8,128)(2,1)}, bf16[1,4096,128]{2,1,0:T(8,128)(2,1)}) fusion(bf16[4,4096,128]{2,1,0:T(8,128)(2,1)} %all-gather.3.cloned.1.call-done), kind=kLoop, calls=%fused_computation.90 | loop fusion | bytes 8388608 | tf_op jit(solution)/shard_map/slice | solution.py:26
  130.3 1.5 copy.83
  131.8 2.3 copy.84
  134.1 2.3 copy.85
  136.4 2.3 copy.86
  138.7 3.5 %fusion.45 = bf16[1,4096,128]{1,2,0:T(8,128)(2,1)} fusion(bf16[1,4096,128]{1,2,0:T(8,128)(2,1)} %copy.86, bf16[1,4096,128]{1,2,0:T(8,128)(2,1)} %copy.85, bf16[1,4096,128]{1,2,0:T(8,128)(2,1)} %copy.84, bf16[1,4096,128]{1,2,0:T(8,128)(2,1)S(1)} %copy.83), kind=kLoop, calls=%fused_computation.54 | loop fusion | flops 4194304 | bytes 5242880 | tf_op jit(solution)/shard_map/convert_element_type | solution.py:22
  142.2 2.3 copy.69
  144.5 48.5 %all-gather.5.cloned.1.call-done = bf16[4,4096,128]{2,1,0:T(8,128)(2,1)} async-done(((bf16[1,4096,128]{2,1,0:T(8,128)(2,1)}), bf16[4,4096,128]{2,1,0:T(8,128)(2,1)}) %all-gather.5.cloned.1.call-update) | async-done | bytes 4194320 | tf_op jit(solution)/shard_map/all_gather | solution.py:22
  193.0 4.3 %fusion.71 = (bf16[1,4096,128]{2,1,0:T(8,128)(2,1)}, bf16[1,4096,128]{2,1,0:T(8,128)(2,1)}, bf16[1,4096,128]{2,1,0:T(8,128)(2,1)}, bf16[1,4096,128]{2,1,0:T(8,128)(2,1)}) fusion(bf16[4,4096,128]{2,1,0:T(8,128)(2,1)} %all-gather.5.cloned.1.call-done), kind=kLoop, calls=%fused_computation.89 | loop fusion | bytes 8388608 | tf_op jit(solution)/shard_map/slice | solution.py:26
  197.3 2.3 copy.87
  199.5 2.3 copy.88
  201.9 2.3 copy.89
  204.1 2.3 copy.90
  206.4 6.0 %fusion.33 = f32[1,4096,128]{1,2,0:T(8,128)} fusion(bf16[1,4096,128]{1,2,0:T(8,128)(2,1)S(1)} %copy.83, bf16[1,4096,128]{1,2,0:T(8,128)(2,1)} %copy.87, bf16[1,4096,128]{1,2,0:T(8,128)(2,1)} %copy.90, bf16[1,4096,128]{1,2,0:T(8,128)(2,1)} %copy.89, bf16[1,4096,128]{1,2,0:T(8,128)(2,1)} %copy.88, bf16[1,4096,128]{1,2,0:T(8,128)(2,1)} %copy.86, ...), kind=kLoop, calls=%fused_computation.41 | loop fusion | flops 12058624 | bytes 10485768 | tf_op jit(solution)/shard_map/add | solution.py:49
  212.5 11.6 %while.25 = (s32[]{:T(128)}, f32[2,512,2,64]{1,3,2,0:T(8,128)S(1)}, f32[2,512,2,64]{1,3,2,0:T(8,128)}, f32[2,4096,2,64]{1,3,2,0:T(8,128)}, f32[4096,2,64]{0,2,1:...) while((s32[]{:T(128)}, f32[2,512,2,64]{1,3,2,0:T(8,128)S(1)}, f32[2,512,2,64]{1,3,2,0:T(8,128)}, ...), condition=%wide.region_4.5_spmd, body=%wide.region_3.4_spmd.sunk | while | flops 546439168 | bytes 49415332 | solution.py:102
  212.5 0.9 bitcast_convert_fusion.4
  213.5 3.3 %multiply_convert_fusion.10 = bf16[512,2,64,64]{0,3,2,1:T(8,128)(2,1)S(1)} fusion(f32[512,2,64]{0,2,1:T(8,128)S(1)} %bitcast_convert_fusion.4), kind=kLoop, calls=%fused_computation.1.clone.1 | loop fusion | flops 8388608 | bytes 8650752 | tf_op jit(solution)/shard_map/while/body/eval_jaxpr/convert_element_type | solution.py:45
  216.8 1.5 fusion.94
  219.3 3.3 %multiply_convert_fusion.10 = bf16[512,2,64,64]{0,3,2,1:T(8,128)(2,1)S(1)} fusion(f32[512,2,64]{0,2,1:T(8,128)S(1)} %bitcast_convert_fusion.4), kind=kLoop, calls=%fused_computation.1.clone.1 | loop fusion | flops 8388608 | bytes 8650752 | tf_op jit(solution)/shard_map/while/body/eval_jaxpr/convert_element_type | solution.py:45
  222.6 1.5 fusion.94
  224.1 1.2 copy.75
  225.5 1.5 reshape.165
  227.3 11.4 %all_to_all.64 = bf16[8,128,128]{1,2,0:T(8,128)(2,1)S(1)} all-to-all(bf16[8,128,128]{1,2,0:T(8,128)(2,1)S(1)} %copy.76), channel_id=1, replica_groups=mesh['aa_0'=4,'aa_1'=4,'ba'=8] {'ba'}, dimensions={0} | all-to-all | bytes 524288 | tf_op jit(solution)/shard_map/all_to_all | solution.py:108
  240.1 9.2 %fusion.46 = bf16[128,1024]{1,0:T(8,128)(2,1)} fusion(f32[128,1024]{1,0:T(8,128)S(1)} %get-tuple-element.207, bf16[4096,1024]{1,0:T(8,128)(2,1)} %param.23, bf16[1024,4096]{1,0:T(8,128)(2,1)} %param.22, f32[1024]{0:T(1024)S(1)} %copy-done.10, f32[128]{0:T(128)S(1)} %add_rsqrt_fusion.1), kind=kOutput, calls=%fused_computation.58 | convolution fusion | flops 2152857600 | bytes 17568256 | tf_op jit(solution)/shard_map/dot_general | solution.py:117
  (65 shorter events, 10.1 us)
Async XLA Ops:
  7.2 232.3 %copy-start = (bf16[1024,1024]{1,0:T(8,128)(2,1)S(1)}, bf16[1024,1024]{1,0:T(8,128)(2,1)}, u32[]{:S(2)}) copy-start(bf16[1024,1024]{1,0:T(8,128)(2,1)} %param.20) | copy-start | bytes 6291460
  7.2 10.3 %copy-start.5 = (bf16[128,1024]{1,0:T(8,128)(2,1)S(1)}, bf16[128,1024]{1,0:T(8,128)(2,1)}, u32[]{:S(2)}) copy-start(bf16[128,1024]{1,0:T(8,128)(2,1)} %param.14) | copy-start | bytes 786436
  7.2 10.3 %copy-start.8 = (f32[1024]{0:T(1024)S(1)}, f32[1024]{0:T(1024)}, u32[]{:S(2)}) copy-start(f32[1024]{0:T(1024)} %param.15) | copy-start | bytes 12292
  11.5 12.4 %all-to-all-start.2 = ((bf16[128,8,128]{0,2,1:T(8,128)(2,1)}), bf16[128,8,128]{0,2,1:T(8,128)(2,1)S(1)}, u32[]{:S(2)}, u32[]{:S(2)}) async-start(bf16[128,8,128]{0,2,1:T(8,128)(2,1)} %bitcast.11), calls=%async_computation.2 | async-start | bytes 524288 | tf_op jit(solution)/shard_map/all_to_all | solution.py:58
  23.9 10.9 %all-to-all-start = ((bf16[128,8,128]{0,2,1:T(8,128)(2,1)}), bf16[128,8,128]{0,2,1:T(8,128)(2,1)S(1)}, u32[]{:S(2)}, u32[]{:S(2)}) async-start(bf16[128,8,128]{0,2,1:T(8,128)(2,1)} %bitcast.7), calls=%async_computation | async-start | bytes 524288 | tf_op jit(solution)/shard_map/all_to_all | solution.py:60
  34.8 10.9 %all-to-all-start.1 = ((bf16[128,8,128]{0,2,1:T(8,128)(2,1)}), bf16[128,8,128]{0,2,1:T(8,128)(2,1)S(1)}, u32[]{:S(2)}, u32[]{:S(2)}) async-start(bf16[128,8,128]{0,2,1:T(8,128)(2,1)} %bitcast.9), calls=%async_computation.1 | async-start | bytes 524288 | tf_op jit(solution)/shard_map/all_to_all | solution.py:59
  39.1 87.0 %all-gather.3.cloned.1.call-start = ((), (), s32[]{:S(2)}) async-start(), calls=%async_computation.4 | async-start | bytes 5242880 | tf_op jit(solution)/shard_map/all_gather | solution.py:22
  49.2 3.3 %copy-start.1 = (f32[4096,2,64]{0,2,1:T(8,128)S(1)}, f32[4096,2,64]{0,2,1:T(8,128)}, u32[]{:S(2)}) copy-start(f32[4096,2,64]{0,2,1:T(8,128)} %get-tuple-element.298) | copy-start | bytes 6291460 | tf_op jit(solution)/shard_map/while
  55.3 1.4 copy-start.2
  62.5 3.3 %copy-start.1 = (f32[4096,2,64]{0,2,1:T(8,128)S(1)}, f32[4096,2,64]{0,2,1:T(8,128)}, u32[]{:S(2)}) copy-start(f32[4096,2,64]{0,2,1:T(8,128)} %get-tuple-element.298) | copy-start | bytes 6291460 | tf_op jit(solution)/shard_map/while
  68.6 1.4 copy-start.2
  71.8 5.2 %copy-start.6 = (f32[2,512,2,64]{1,3,2,0:T(8,128)}, f32[2,512,2,64]{1,3,2,0:T(8,128)S(1)}, u32[]{:S(2)}) copy-start(f32[2,512,2,64]{1,3,2,0:T(8,128)S(1)} %get-tuple-element.317) | copy-start | bytes 1572868
  77.0 116.0 %all-gather.5.cloned.1.call-start = ((), (), s32[]{:S(2)}) async-start(), calls=%async_computation.5 | async-start | bytes 5242880 | tf_op jit(solution)/shard_map/all_gather | solution.py:22
  213.5 3.3 %copy-start.3 = (f32[4096,2,64]{0,2,1:T(8,128)S(1)}, f32[4096,2,64]{0,2,1:T(8,128)}, u32[]{:S(2)}) copy-start(f32[4096,2,64]{0,2,1:T(8,128)} %get-tuple-element.333) | copy-start | bytes 6291460 | tf_op jit(solution)/shard_map/while
  213.5 3.3 %copy-start.4 = (f32[2,4096,2,64]{1,3,2,0:T(8,128)S(1)}, f32[2,4096,2,64]{1,3,2,0:T(8,128)}, u32[]{:S(2)}) copy-start(f32[2,4096,2,64]{1,3,2,0:T(8,128)} %get-tuple-element.332) | copy-start | bytes 12582916 | tf_op jit(solution)/shard_map/while
  213.5 3.3 %copy-start.7 = (f32[2,512,2,64]{1,3,2,0:T(8,128)S(1)}, f32[2,512,2,64]{1,3,2,0:T(8,128)}, u32[]{:S(2)}) copy-start(f32[2,512,2,64]{1,3,2,0:T(8,128)} %get-tuple-element.331) | copy-start | bytes 1572868 | tf_op jit(solution)/shard_map/while
  219.2 3.3 %copy-start.3 = (f32[4096,2,64]{0,2,1:T(8,128)S(1)}, f32[4096,2,64]{0,2,1:T(8,128)}, u32[]{:S(2)}) copy-start(f32[4096,2,64]{0,2,1:T(8,128)} %get-tuple-element.333) | copy-start | bytes 6291460 | tf_op jit(solution)/shard_map/while
  219.2 3.3 %copy-start.4 = (f32[2,4096,2,64]{1,3,2,0:T(8,128)S(1)}, f32[2,4096,2,64]{1,3,2,0:T(8,128)}, u32[]{:S(2)}) copy-start(f32[2,4096,2,64]{1,3,2,0:T(8,128)} %get-tuple-element.332) | copy-start | bytes 12582916 | tf_op jit(solution)/shard_map/while
  219.3 3.3 %copy-start.7 = (f32[2,512,2,64]{1,3,2,0:T(8,128)S(1)}, f32[2,512,2,64]{1,3,2,0:T(8,128)}, u32[]{:S(2)}) copy-start(f32[2,512,2,64]{1,3,2,0:T(8,128)} %get-tuple-element.331) | copy-start | bytes 1572868 | tf_op jit(solution)/shard_map/while
  224.1 2.9 %copy-start.9 = (f32[128]{0:T(128)S(1)}, f32[128]{0:T(128)}, u32[]{:S(2)}) copy-start(f32[128]{0:T(128)} %param.19) | copy-start | bytes 1540
  227.2 12.8 %copy-start.10 = (f32[1024]{0:T(1024)S(1)}, f32[1024]{0:T(1024)}, u32[]{:S(2)}) copy-start(f32[1024]{0:T(1024)} %param.21) | copy-start | bytes 12292
Sparse Core Ops, SparseCore 0:
  77.1 48.9 all-gather.2
  144.6 48.3 all-gather.4
where the time goes:
time: 257 us; the launch traced here: 256 us
  waiting for transfers between devices  110 us (43%)
  local copies, waits for them, and re-layouts  42 us (16%)
  other arithmetic  35.6 us (14%)
  matrix products  28 us (11%)
  starting transfers between devices  14.9 us (6%)
  between operations  14.3 us (6%)
  blocking collectives  11.4 us (4%)
    all_gather x2, waiting for transfers between devices, prefix_by_axis(): pieces = lax.all_gather(subtotal.astype(jnp.bfloat16), axis)  97.4 us
    unnamed x25, local copies, waits for them, and re-layouts  20 us
    convert_element_type x4, other arithmetic, features(): return outer_features(vectors).astype(jnp.bfloat16)  13.2 us
    all_to_all x1, blocking collectives, body(): lax.all_to_all(attended_heads, 'ba', split_axis=0, concat_axis=1, tiled=T...  11.4 us
    dot_general x1, matrix products, body(): jnp.dot(hidden, w_out, preferred_element_type=jnp.float32)  9.17 us
    slice x2, local copies, waits for them, and re-layouts, prefix_by_axis(): subtotal = combine(subtotal, pieces[k].astype(shard.dtype))  8.52 us
    convert_element_type x2, other arithmetic, prefix_by_axis(): pieces = lax.all_gather(subtotal.astype(jnp.bfloat16), axis)  6.37 us
    add x1, other arithmetic, add_states(): return earlier_state + later_state  6.04 us
  transfers between devices with their start and end apart: 5, of which 5 were waited for; matrix products, arithmetic and copies ran while one was open for 3% of the time, Pallas kernels for 0%

commit v1 on v0

--- a/solution.py
+++ b/solution.py
@@ -8,6 +8,12 @@
 H = 16
 AA = ("aa_0", "aa_1")
 AA_BA = ("aa_0", "aa_1", "ba")
+
+
+def entries_proceed(slab_in):
+    return jnp.concatenate(
+        lax.all_to_all(jnp.stack(jnp.split(slab_in, lax.axis_size("ba"), 1), 0), "ba", 0, 0), axis=0
+    )
 
 
 def neutral_like(shard, identity):
@@ -56,7 +62,7 @@
     values_loc = jnp.dot(normed, w_value, preferred_element_type=jnp.float32).astype(jnp.bfloat16)
     queries, keys, values = (
         lax.all_to_all(query_loc, "ba", split_axis=1, concat_axis=0, tiled=True),
-        lax.all_to_all(keys_loc, "ba", split_axis=1, concat_axis=0, tiled=True),
+        entries_proceed(keys_loc),
         lax.all_to_all(values_loc, "ba", split_axis=1, concat_axis=0, tiled=True),
     )
     head_size = D // H

time: 257 us -> 261 us (1.016)
  local copies, waits for them, and re-layouts: 42 us -> 47.7 us
    unnamed x25 -> x34, local copies, waits for them, and re-layouts: 20 us -> 25 us
  transfers between devices with their start and end apart: 5 -> 5, of which waited for: 5 -> 5; matrix products, arithmetic and copies ran while one was open for 3% -> 4% of each run, Pallas kernels for 0% -> 0%
where the time goes in v1:
time: 261 us; the launch traced here: 260 us
  waiting for transfers between devices  108 us (41%)
  local copies, waits for them, and re-layouts  47.7 us (18%)
  other arithmetic  35.6 us (14%)
  matrix products  28 us (11%)
  starting transfers between devices  14.9 us (6%)
  between operations  14.3 us (5%)
  blocking collectives  11.4 us (4%)
    all_gather x2, waiting for transfers between devices, prefix_by_axis(): pieces = lax.all_gather(subtotal.astype(jnp.bfloat16), axis)  97.4 us
    unnamed x34, local copies, waits for them, and re-layouts  25 us
    convert_element_type x4, other arithmetic, features(): return outer_features(vectors).astype(jnp.bfloat16)  13.2 us
    all_to_all x1, blocking collectives, body(): lax.all_to_all(attended_heads, 'ba', split_axis=0, concat_axis=1, tiled=T...  11.4 us
    dot_general x1, matrix products, body(): jnp.dot(hidden, w_out, preferred_element_type=jnp.float32)  9.17 us
    slice x2, local copies, waits for them, and re-layouts, prefix_by_axis(): subtotal = combine(subtotal, pieces[k].astype(shard.dtype))  8.5 us
    convert_element_type x2, other arithmetic, prefix_by_axis(): pieces = lax.all_gather(subtotal.astype(jnp.bfloat16), axis)  6.38 us
    add x1, other arithmetic, add_states(): return earlier_state + later_state  6.04 us
  transfers between devices with their start and end apart: 5, of which 5 were waited for; matrix products, arithmetic and copies ran while one was open for 4% of the time, Pallas kernels for 0%

profile of v1, /device:TPU:1, one launch (start us, length us, event | category | flops | bytes accessed | tf_op | source)
XLA Modules:
  0.0 259.9 jit_solution(15991340621586540281)
XLA Ops:
  7.2 1.2 fusion.54
  8.4 2.2 convolution_convert_fusion.1
  15.7 6.0 %all-to-all-start.1 = ((bf16[8,128,128]{2,1,0:T(8,128)(2,1)}), bf16[8,128,128]{2,1,0:T(8,128)(2,1)S(1)}, u32[]{:S(2)}, u32[]{:S(2)}) async-start(bf16[8,128,128]{2,1,0:T(8,128)(2,1)} %fusion.64), calls=%async_computation.1 | async-start | bytes 524288 | tf_op jit(solution)/shard_map/all_to_all | solution.py:15
  21.6 2.1 convolution_convert_fusion
  24.6 3.5 %all-to-all-done.1 = bf16[8,128,128]{2,1,0:T(8,128)(2,1)S(1)} async-done(((bf16[8,128,128]{2,1,0:T(8,128)(2,1)}), bf16[8,128,128]{2,1,0:T(8,128)(2,1)S(1)}, u32[]{:S(2)}, u32[]{:S(2)}) %all-to-all-start.1) | async-done | bytes 262176 | tf_op jit(solution)/shard_map/all_to_all | solution.py:15
  28.1 4.4 %all-to-all-start.2 = ((bf16[128,8,128]{0,2,1:T(8,128)(2,1)}), bf16[128,8,128]{0,2,1:T(8,128)(2,1)S(1)}, u32[]{:S(2)}, u32[]{:S(2)}) async-start(bf16[128,8,128]{0,2,1:T(8,128)(2,1)} %bitcast.17), calls=%async_computation.2 | async-start | bytes 524288 | tf_op jit(solution)/shard_map/all_to_all | solution.py:64
  32.4 2.1 convolution_convert_fusion.2
  35.4 3.6 %all-to-all-done.2 = bf16[128,8,128]{0,2,1:T(8,128)(2,1)S(1)} async-done(((bf16[128,8,128]{0,2,1:T(8,128)(2,1)}), bf16[128,8,128]{0,2,1:T(8,128)(2,1)S(1)}, u32[]{:S(2)}, u32[]{:S(2)}) %all-to-all-start.2) | async-done | bytes 262176 | tf_op jit(solution)/shard_map/all_to_all | solution.py:64
  38.9 4.4 %all-to-all-start = ((bf16[128,8,128]{0,2,1:T(8,128)(2,1)}), bf16[128,8,128]{0,2,1:T(8,128)(2,1)S(1)}, u32[]{:S(2)}, u32[]{:S(2)}) async-start(bf16[128,8,128]{0,2,1:T(8,128)(2,1)} %bitcast.7), calls=%async_computation | async-start | bytes 524288 | tf_op jit(solution)/shard_map/all_to_all | solution.py:66
  44.6 1.1 copy.59
  46.6 3.2 %all-to-all-done = bf16[128,8,128]{0,2,1:T(8,128)(2,1)S(1)} async-done(((bf16[128,8,128]{0,2,1:T(8,128)(2,1)}), bf16[128,8,128]{0,2,1:T(8,128)(2,1)S(1)}, u32[]{:S(2)}, u32[]{:S(2)}) %all-to-all-start) | async-done | bytes 262176 | tf_op jit(solution)/shard_map/all_to_all | solution.py:66
  50.2 25.0 %while.26 = (s32[]{:T(128)}, f32[4096,2,64]{0,2,1:T(8,128)}, f32[2,512,2,64]{1,3,2,0:T(8,128)S(1)}, f32[2,4096,2,64]{1,3,2,0:T(8,128)}, bf16[2,512,2,64]{1,3,2,0...) while((s32[]{:T(128)}, f32[4096,2,64]{0,2,1:T(8,128)}, ...), condition=%wide.region_2.3_spmd.clone, body=%wide.region_1.2_spmd.clone.sunk | while | flops 682950656 | bytes 43911844 | solution.py:92
  50.2 1.6 bitcast_dynamic-update-slice_fusion.2
  52.7 3.3 %multiply_convert_fusion.11 = bf16[512,2,64,64]{0,3,2,1:T(8,128)(2,1)S(1)} fusion(f32[512,2,64]{0,2,1:T(8,128)S(1)} %bitcast_convert_fusion.5), kind=kLoop, calls=%fused_computation.10.clone.1 | loop fusion | flops 8388608 | bytes 8650752 | tf_op jit(solution)/shard_map/while/body/eval_jaxpr/convert_element_type | solution.py:51
  56.0 2.8 %fusion.108 = f32[4096,2,64]{0,2,1:T(8,128)S(1)} fusion(bf16[512,2,4096]{0,2,1:T(8,128)(2,1)S(1)} %bitcast.151, f32[4096,2,64]{0,2,1:T(8,128)S(1)} %copy-done.1, pred[]{:T(512)S(6)} %compare.3, bf16[2,512,2,64]{1,3,2,0:T(8,128)(2,1)S(1)} %get-tuple-element.317, s32[]{:T(128)} %get-tuple-element.304), kind=kOutput, calls=%fused_computation.12.clone.1 | convolution fusion | flops 537919488 | bytes 12713989 | tf_op jit(solution)/shard_map/while/body/eval_jaxpr/jhf,jhd->fhd/dot_general | solution.py:85
  58.8 1.3 copy-done.2
  60.2 1.7 fusion.109
  61.9 3.1 %bitcast_dynamic-update-slice_fusion.2 = f32[2,4096,2,64]{1,3,2,0:T(8,128)} fusion(f32[2,4096,2,64]{1,3,2,0:T(8,128)} %get-tuple-element.307, s32[]{:T(128)} %get-tuple-element.304, f32[4096,2,64]{0,2,1:T(8,128)} %get-tuple-element.305, pred[]{:T(512)S(6)} %compare.3), kind=kLoop, calls=%fused_computation.13.clone.1 | loop fusion | flops 524288 | bytes 4194817 | tf_op jit(solution)/shard_map/while/body/jit(dynamic_update_index_in_dim)/dynamic_update_slice | solution.py:92
  66.0 3.3 %multiply_convert_fusion.11 = bf16[512,2,64,64]{0,3,2,1:T(8,128)(2,1)S(1)} fusion(f32[512,2,64]{0,2,1:T(8,128)S(1)} %bitcast_convert_fusion.5), kind=kLoop, calls=%fused_computation.10.clone.1 | loop fusion | flops 8388608 | bytes 8650752 | tf_op jit(solution)/shard_map/while/body/eval_jaxpr/convert_element_type | solution.py:51
  69.3 2.8 %fusion.108 = f32[4096,2,64]{0,2,1:T(8,128)S(1)} fusion(bf16[512,2,4096]{0,2,1:T(8,128)(2,1)S(1)} %bitcast.151, f32[4096,2,64]{0,2,1:T(8,128)S(1)} %copy-done.1, pred[]{:T(512)S(6)} %compare.3, bf16[2,512,2,64]{1,3,2,0:T(8,128)(2,1)S(1)} %get-tuple-element.317, s32[]{:T(128)} %get-tuple-element.304), kind=kOutput, calls=%fused_computation.12.clone.1 | convolution fusion | flops 537919488 | bytes 12713989 | tf_op jit(solution)/shard_map/while/body/eval_jaxpr/jhf,jhd->fhd/dot_general | solution.py:85
  72.1 1.3 copy-done.2
  73.5 1.7 fusion.109
  75.2 2.9 %convert_element_type.145 = bf16[4096,2,64]{0,2,1:T(8,128)(2,1)} convert(f32[4096,2,64]{0,2,1:T(8,128)} %get-tuple-element.80) | non-fusion elementwise | flops 524288 | bytes 3145728 | tf_op jit(solution)/shard_map/convert_element_type | solution.py:28
  78.1 2.3 copy.63
  80.7 48.9 %all-gather.3.cloned.1.call-done = bf16[4,4096,128]{2,1,0:T(8,128)(2,1)} async-done(((bf16[1,4096,128]{2,1,0:T(8,128)(2,1)}), bf16[4,4096,128]{2,1,0:T(8,128)(2,1)}) %all-gather.3.cloned.1.call-update) | async-done | bytes 4194320 | tf_op jit(solution)/shard_map/all_gather | solution.py:28
  129.6 4.2 %fusion.80 = (bf16[1,4096,128]{2,1,0:T(8,128)(2,1)}, bf16[1,4096,128]{2,1,0:T(8,128)(2,1)}, bf16[1,4096,128]{2,1,0:T(8,128)(2,1)}, bf16[1,4096,128]{2,1,0:T(8,128)(2,1)}) fusion(bf16[4,4096,128]{2,1,0:T(8,128)(2,1)} %all-gather.3.cloned.1.call-done), kind=kLoop, calls=%fused_computation.106 | loop fusion | bytes 8388608 | tf_op jit(solution)/shard_map/slice | solution.py:32
  133.8 1.5 copy.83
  135.3 2.3 copy.84
  137.6 2.3 copy.85
  139.9 2.3 copy.86
  142.2 3.5 %fusion.45 = bf16[1,4096,128]{1,2,0:T(8,128)(2,1)} fusion(bf16[1,4096,128]{1,2,0:T(8,128)(2,1)} %copy.86, bf16[1,4096,128]{1,2,0:T(8,128)(2,1)} %copy.85, bf16[1,4096,128]{1,2,0:T(8,128)(2,1)} %copy.84, bf16[1,4096,128]{1,2,0:T(8,128)(2,1)S(1)} %copy.83), kind=kLoop, calls=%fused_computation.54 | loop fusion | flops 4194304 | bytes 5242880 | tf_op jit(solution)/shard_map/convert_element_type | solution.py:28
  145.7 2.3 copy.68
  148.1 48.5 %all-gather.5.cloned.1.call-done = bf16[4,4096,128]{2,1,0:T(8,128)(2,1)} async-done(((bf16[1,4096,128]{2,1,0:T(8,128)(2,1)}), bf16[4,4096,128]{2,1,0:T(8,128)(2,1)}) %all-gather.5.cloned.1.call-update) | async-done | bytes 4194320 | tf_op jit(solution)/shard_map/all_gather | solution.py:28
  196.5 4.3 %fusion.79 = (bf16[1,4096,128]{2,1,0:T(8,128)(2,1)}, bf16[1,4096,128]{2,1,0:T(8,128)(2,1)}, bf16[1,4096,128]{2,1,0:T(8,128)(2,1)}, bf16[1,4096,128]{2,1,0:T(8,128)(2,1)}) fusion(bf16[4,4096,128]{2,1,0:T(8,128)(2,1)} %all-gather.5.cloned.1.call-done), kind=kLoop, calls=%fused_computation.105 | loop fusion | bytes 8388608 | tf_op jit(solution)/shard_map/slice | solution.py:32
  200.9 2.3 copy.87
  203.2 2.4 copy.88
  205.6 2.3 copy.89
  207.9 2.3 copy.90
  210.2 6.0 %fusion.33 = f32[1,4096,128]{1,2,0:T(8,128)} fusion(bf16[1,4096,128]{1,2,0:T(8,128)(2,1)S(1)} %copy.83, bf16[1,4096,128]{1,2,0:T(8,128)(2,1)} %copy.87, bf16[1,4096,128]{1,2,0:T(8,128)(2,1)} %copy.90, bf16[1,4096,128]{1,2,0:T(8,128)(2,1)} %copy.89, bf16[1,4096,128]{1,2,0:T(8,128)(2,1)} %copy.88, bf16[1,4096,128]{1,2,0:T(8,128)(2,1)} %copy.86, ...), kind=kLoop, calls=%fused_computation.41 | loop fusion | flops 12058624 | bytes 10485768 | tf_op jit(solution)/shard_map/add | solution.py:55
  216.3 11.6 %while.25 = (s32[]{:T(128)}, f32[2,512,2,64]{1,3,2,0:T(8,128)S(1)}, f32[2,512,2,64]{1,3,2,0:T(8,128)}, f32[2,4096,2,64]{1,3,2,0:T(8,128)}, f32[4096,2,64]{0,2,1:...) while((s32[]{:T(128)}, f32[2,512,2,64]{1,3,2,0:T(8,128)S(1)}, f32[2,512,2,64]{1,3,2,0:T(8,128)}, ...), condition=%wide.region_4.5_spmd, body=%wide.region_3.4_spmd.sunk | while | flops 546439168 | bytes 49415332 | solution.py:108
  217.3 3.3 %multiply_convert_fusion.10 = bf16[512,2,64,64]{0,3,2,1:T(8,128)(2,1)S(1)} fusion(f32[512,2,64]{0,2,1:T(8,128)S(1)} %bitcast_convert_fusion.4), kind=kLoop, calls=%fused_computation.1.clone.1 | loop fusion | flops 8388608 | bytes 8650752 | tf_op jit(solution)/shard_map/while/body/eval_jaxpr/convert_element_type | solution.py:51
  220.6 1.5 fusion.102
  223.1 3.3 %multiply_convert_fusion.10 = bf16[512,2,64,64]{0,3,2,1:T(8,128)(2,1)S(1)} fusion(f32[512,2,64]{0,2,1:T(8,128)S(1)} %bitcast_convert_fusion.4), kind=kLoop, calls=%fused_computation.1.clone.1 | loop fusion | flops 8388608 | bytes 8650752 | tf_op jit(solution)/shard_map/while/body/eval_jaxpr/convert_element_type | solution.py:51
  226.4 1.5 fusion.102
  227.9 1.2 copy.74
  229.3 1.5 reshape.157
  231.0 11.4 %all_to_all.53 = bf16[8,128,128]{1,2,0:T(8,128)(2,1)S(1)} all-to-all(bf16[8,128,128]{1,2,0:T(8,128)(2,1)S(1)} %copy.75), channel_id=1, replica_groups=mesh['aa_0'=4,'aa_1'=4,'ba'=8] {'ba'}, dimensions={0} | all-to-all | bytes 524288 | tf_op jit(solution)/shard_map/all_to_all | solution.py:114
  243.9 9.2 %fusion.46 = bf16[128,1024]{1,0:T(8,128)(2,1)} fusion(f32[128,1024]{1,0:T(8,128)S(1)} %get-tuple-element.214, bf16[4096,1024]{1,0:T(8,128)(2,1)} %param.23, bf16[1024,4096]{1,0:T(8,128)(2,1)} %param.22, f32[1024]{0:T(1024)S(1)} %copy-done.11, f32[128]{0:T(128)S(1)} %add_rsqrt_fusion.1), kind=kOutput, calls=%fused_computation.58 | convolution fusion | flops 2152857600 | bytes 17568256 | tf_op jit(solution)/shard_map/dot_general | solution.py:123
  (73 shorter events, 15.3 us)
Async XLA Ops:
  7.2 236.1 %copy-start = (bf16[1024,1024]{1,0:T(8,128)(2,1)S(1)}, bf16[1024,1024]{1,0:T(8,128)(2,1)}, u32[]{:S(2)}) copy-start(bf16[1024,1024]{1,0:T(8,128)(2,1)} %param.20) | copy-start | bytes 6291460
  7.2 14.4 %copy-start.5 = (bf16[128,1024]{1,0:T(8,128)(2,1)S(1)}, bf16[128,1024]{1,0:T(8,128)(2,1)}, u32[]{:S(2)}) copy-start(bf16[128,1024]{1,0:T(8,128)(2,1)} %param.14) | copy-start | bytes 786436
  7.2 14.4 %copy-start.9 = (f32[1024]{0:T(1024)S(1)}, f32[1024]{0:T(1024)}, u32[]{:S(2)}) copy-start(f32[1024]{0:T(1024)} %param.15) | copy-start | bytes 12292
  15.7 12.4 %all-to-all-start.1 = ((bf16[8,128,128]{2,1,0:T(8,128)(2,1)}), bf16[8,128,128]{2,1,0:T(8,128)(2,1)S(1)}, u32[]{:S(2)}, u32[]{:S(2)}) async-start(bf16[8,128,128]{2,1,0:T(8,128)(2,1)} %fusion.64), calls=%async_computation.1 | async-start | bytes 524288 | tf_op jit(solution)/shard_map/all_to_all | solution.py:15
  28.1 10.9 %all-to-all-start.2 = ((bf16[128,8,128]{0,2,1:T(8,128)(2,1)}), bf16[128,8,128]{0,2,1:T(8,128)(2,1)S(1)}, u32[]{:S(2)}, u32[]{:S(2)}) async-start(bf16[128,8,128]{0,2,1:T(8,128)(2,1)} %bitcast.17), calls=%async_computation.2 | async-start | bytes 524288 | tf_op jit(solution)/shard_map/all_to_all | solution.py:64
  38.9 4.4 %copy-start.8 = (bf16[128,8,128]{0,2,1:T(8,128)(2,1)}, bf16[128,8,128]{0,2,1:T(8,128)(2,1)S(1)}, u32[]{:S(2)}) copy-start(bf16[128,8,128]{0,2,1:T(8,128)(2,1)S(1)} %all-to-all-done.2) | copy-start | bytes 786436
  38.9 10.9 %all-to-all-start = ((bf16[128,8,128]{0,2,1:T(8,128)(2,1)}), bf16[128,8,128]{0,2,1:T(8,128)(2,1)S(1)}, u32[]{:S(2)}, u32[]{:S(2)}) async-start(bf16[128,8,128]{0,2,1:T(8,128)(2,1)} %bitcast.7), calls=%async_computation | async-start | bytes 524288 | tf_op jit(solution)/shard_map/all_to_all | solution.py:66
  43.3 86.3 %all-gather.3.cloned.1.call-start = ((), (), s32[]{:S(2)}) async-start(), calls=%async_computation.4 | async-start | bytes 5242880 | tf_op jit(solution)/shard_map/all_gather | solution.py:28
  52.7 3.3 %copy-start.1 = (f32[4096,2,64]{0,2,1:T(8,128)S(1)}, f32[4096,2,64]{0,2,1:T(8,128)}, u32[]{:S(2)}) copy-start(f32[4096,2,64]{0,2,1:T(8,128)} %get-tuple-element.305) | copy-start | bytes 6291460 | tf_op jit(solution)/shard_map/while
  58.7 1.4 copy-start.2
  66.0 3.3 %copy-start.1 = (f32[4096,2,64]{0,2,1:T(8,128)S(1)}, f32[4096,2,64]{0,2,1:T(8,128)}, u32[]{:S(2)}) copy-start(f32[4096,2,64]{0,2,1:T(8,128)} %get-tuple-element.305) | copy-start | bytes 6291460 | tf_op jit(solution)/shard_map/while
  72.0 1.4 copy-start.2
  75.2 5.2 %copy-start.6 = (f32[2,512,2,64]{1,3,2,0:T(8,128)}, f32[2,512,2,64]{1,3,2,0:T(8,128)S(1)}, u32[]{:S(2)}) copy-start(f32[2,512,2,64]{1,3,2,0:T(8,128)S(1)} %get-tuple-element.324) | copy-start | bytes 1572868
  80.5 116.1 %all-gather.5.cloned.1.call-start = ((), (), s32[]{:S(2)}) async-start(), calls=%async_computation.5 | async-start | bytes 5242880 | tf_op jit(solution)/shard_map/all_gather | solution.py:28
  217.2 3.3 %copy-start.3 = (f32[4096,2,64]{0,2,1:T(8,128)S(1)}, f32[4096,2,64]{0,2,1:T(8,128)}, u32[]{:S(2)}) copy-start(f32[4096,2,64]{0,2,1:T(8,128)} %get-tuple-element.340) | copy-start | bytes 6291460 | tf_op jit(solution)/shard_map/while
  217.3 3.3 %copy-start.4 = (f32[2,4096,2,64]{1,3,2,0:T(8,128)S(1)}, f32[2,4096,2,64]{1,3,2,0:T(8,128)}, u32[]{:S(2)}) copy-start(f32[2,4096,2,64]{1,3,2,0:T(8,128)} %get-tuple-element.339) | copy-start | bytes 12582916 | tf_op jit(solution)/shard_map/while
  217.3 3.3 %copy-start.7 = (f32[2,512,2,64]{1,3,2,0:T(8,128)S(1)}, f32[2,512,2,64]{1,3,2,0:T(8,128)}, u32[]{:S(2)}) copy-start(f32[2,512,2,64]{1,3,2,0:T(8,128)} %get-tuple-element.338) | copy-start | bytes 1572868 | tf_op jit(solution)/shard_map/while
  223.0 3.3 %copy-start.3 = (f32[4096,2,64]{0,2,1:T(8,128)S(1)}, f32[4096,2,64]{0,2,1:T(8,128)}, u32[]{:S(2)}) copy-start(f32[4096,2,64]{0,2,1:T(8,128)} %get-tuple-element.340) | copy-start | bytes 6291460 | tf_op jit(solution)/shard_map/while
  223.0 3.3 %copy-start.4 = (f32[2,4096,2,64]{1,3,2,0:T(8,128)S(1)}, f32[2,4096,2,64]{1,3,2,0:T(8,128)}, u32[]{:S(2)}) copy-start(f32[2,4096,2,64]{1,3,2,0:T(8,128)} %get-tuple-element.339) | copy-start | bytes 12582916 | tf_op jit(solution)/shard_map/while
  223.0 3.3 %copy-start.7 = (f32[2,512,2,64]{1,3,2,0:T(8,128)S(1)}, f32[2,512,2,64]{1,3,2,0:T(8,128)}, u32[]{:S(2)}) copy-start(f32[2,512,2,64]{1,3,2,0:T(8,128)} %get-tuple-element.338) | copy-start | bytes 1572868 | tf_op jit(solution)/shard_map/while
  227.9 2.9 %copy-start.10 = (f32[128]{0:T(128)S(1)}, f32[128]{0:T(128)}, u32[]{:S(2)}) copy-start(f32[128]{0:T(128)} %param.19) | copy-start | bytes 1540
  231.0 12.8 %copy-start.11 = (f32[1024]{0:T(1024)S(1)}, f32[1024]{0:T(1024)}, u32[]{:S(2)}) copy-start(f32[1024]{0:T(1024)} %param.21) | copy-start | bytes 12292
Sparse Core Ops, SparseCore 0:
  80.6 48.9 all-gather.2
  148.2 48.3 all-gather.4
